TPU v7x, 512 devices: a whole 4x4x16 slice. The times are simulated.
512 devices in a mesh: row: 16 (over y, x), col: 32 (over z, core).
Axes of the slice: x: 4, y: 4, z: 16, core: 2. Of those that a mesh axis runs over, the one named last changes fastest.
Arguments:
- out_grad: bfloat16 [2048, 8192], P('col', 'row'), may hold values from -6 to 6
- hidden: bfloat16 [2048, 28672], P('row', 'col'), may hold values from -0.12988281 to 0.12988281
- weight: bfloat16 [28672, 8192], P('col', 'row'), may hold values from -0.03125 to 0.03125
Outputs:
- token_grad: bfloat16 [2048, 28672], P('row', 'col')
- weight_grad: bfloat16 [28672, 8192], P('col', 'row')
All inputs are finite; a program needn't handle non-finite values.
Results may differ from a plain program's by a relative error of at most 0.001.
Values may be sent and summed in bfloat16 or wider, within the bound.
A program may use at most 64 MiB of HBM per device.

v0:
```python
import jax
import jax.numpy as jnp
from jax import lax
from jax.sharding import PartitionSpec as P


def on_device(out_grad, hidden, weight):
    gathered = lax.all_gather(out_grad, "col", axis=0, tiled=True)
    cotangent = gathered
    weight_sum = lax.dot_general(
        lax.all_gather(hidden, "row", axis=0, tiled=True),
        cotangent,
        (((0,), (0,)), ((), ())),
        preferred_element_type=jnp.float32,
    )
    weight_grad = weight_sum.astype(jnp.bfloat16)
    own_full = lax.all_to_all(gathered, "row", split_axis=0, concat_axis=1, tiled=True)
    cotangent = own_full
    token_sum = lax.dot_general(
        cotangent,
        lax.all_gather(weight, "row", axis=1, tiled=True),
        (((1,), (1,)), ((), ())),
        preferred_element_type=jnp.float32,
    )
    return (token_sum.astype(jnp.bfloat16), weight_grad)


def solution(mesh):
    return jax.shard_map(
        on_device,
        mesh=mesh,
        in_specs=(P("col", "row"), P("row", "col"), P("col", "row")),
        out_specs=(P("row", "col"), P("col", "row")),
        check_vma=False,
    )
```

profile of v0, /device:TPU:1, one launch (start us, length us, event | category | flops | bytes accessed | tf_op | source)
XLA Modules:
  0.0 301.2 jit_solution(12447496459693819890)
XLA Ops:
  7.2 0.0 all-gather.4.cloned.1.call-start
  7.2 0.7 all-gather.4.cloned.1.call-update
  7.9 0.0 all-gather.8.cloned.1.call-start
  7.9 0.7 all-gather.8.cloned.1.call-update
  8.6 0.0 all-gather.6.cloned.1.call-start
  8.7 0.7 all-gather.6.cloned.1.call-update
  9.4 78.3 %all-gather.4.cloned.1.call-done = bf16[2048,512]{1,0:T(8,128)(2,1)} async-done(((bf16[64,512]{1,0:T(8,128)(2,1)}), bf16[2048,512]{1,0:T(8,128)(2,1)}) %all-gather.4.cloned.1.call-update) | async-done | bytes 2097168 | tf_op jit(solution)/shard_map/all_gather | solution.py:8
  87.7 37.9 %all_to_all.19 = bf16[16,128,512]{2,1,0:T(8,128)(2,1)S(1)} all-to-all(bf16[16,128,512]{2,1,0:T(8,128)(2,1)} %bitcast.9), channel_id=1, replica_groups=mesh['row'=16,'col'=32] {'row'}, dimensions={0} | all-to-all | bytes 4194304 | tf_op jit(solution)/shard_map/all_to_all | solution.py:17
  125.6 2.4 copy.5
  127.9 0.0 copy-start
  127.9 28.6 %all-gather.8.cloned.1.call-done = bf16[2048,896]{1,0:T(8,128)(2,1)} async-done(((bf16[128,896]{1,0:T(8,128)(2,1)}), bf16[2048,896]{1,0:T(8,128)(2,1)}) %all-gather.8.cloned.1.call-update) | async-done | bytes 3670032 | tf_op jit(solution)/shard_map/all_gather | solution.py:11
  156.6 5.7 %convolution_convert_fusion = bf16[896,512]{1,0:T(8,128)(2,1)} fusion(bf16[2048,896]{1,0:T(8,128)(2,1)} %all-gather.8.cloned.1.call-done, bf16[2048,512]{1,0:T(8,128)(2,1)} %all-gather.4.cloned.1.call-done), kind=kOutput, calls=%fused_computation | convolution fusion | flops 1879506944 | bytes 6684672 | tf_op jit(solution)/shard_map/dot_general | solution.py:10
  162.3 121.8 %all-gather.6.cloned.1.call-done = bf16[896,8192]{1,0:T(8,128)(2,1)} async-done(((bf16[896,512]{1,0:T(8,128)(2,1)}), bf16[896,8192]{1,0:T(8,128)(2,1)}) %all-gather.6.cloned.1.call-update) | async-done | bytes 14680080 | tf_op jit(solution)/shard_map/all_gather | solution.py:21
  284.1 0.0 copy-done
  284.1 10.6 %convolution_convert_fusion.1 = bf16[128,896]{1,0:T(8,128)(2,1)} fusion(bf16[128,8192]{0,1:T(8,128)(2,1)S(1)} %bitcast.8, bf16[896,8192]{1,0:T(8,128)(2,1)} %all-gather.6.cloned.1.call-done), kind=kOutput, calls=%fused_computation.1 | convolution fusion | flops 1879162880 | bytes 17006592 | tf_op jit(solution)/shard_map/dot_general | solution.py:19
Async XLA Ops:
  7.2 80.5 %all-gather.4.cloned.1.call-start = ((), (), s32[]{:S(2)}) async-start(), calls=%async_computation.1 | async-start | bytes 2162688 | tf_op jit(solution)/shard_map/all_gather | solution.py:8
  7.9 148.7 %all-gather.8.cloned.1.call-start = ((), (), s32[]{:S(2)}) async-start(), calls=%async_computation.3 | async-start | bytes 3899392 | tf_op jit(solution)/shard_map/all_gather | solution.py:11
  8.6 275.4 %all-gather.6.cloned.1.call-start = ((), (), s32[]{:S(2)}) async-start(), calls=%async_computation.2 | async-start | bytes 15597568 | tf_op jit(solution)/shard_map/all_gather | solution.py:21
  127.9 156.1 %copy-start = (bf16[128,16,512]{0,2,1:T(8,128)(2,1)S(1)}, bf16[128,16,512]{0,2,1:T(8,128)(2,1)}, u32[]{:S(2)}) copy-start(bf16[128,16,512]{0,2,1:T(8,128)(2,1)} %copy.5) | copy-start | bytes 6291460
Sparse Core Ops, SparseCore 0:
  10.1 77.5 all-gather.3
  90.7 65.8 all-gather.7
  159.6 124.4 all-gather.5
where the time goes:
time: 301 us
  waiting for transfers between devices  231 us (77%)
  blocking collectives  37.9 us (13%)
  matrix products  16.3 us (5%)
  between operations  13.7 us (5%)
    all_gather x1, waiting for transfers between devices, on_device(): lax.all_gather(weight, 'row', axis=1, tiled=True)  122 us
    all_gather x1, waiting for transfers between devices, on_device(): gathered = lax.all_gather(out_grad, 'col', axis=0, tiled=True)  78.3 us
    all_to_all x1, blocking collectives, on_device(): lax.all_to_all(gathered, 'row', split_axis=0, concat_axis=1, tiled=True)  37.9 us
    all_gather x1, waiting for transfers between devices, on_device(): lax.all_gather(hidden, 'row', axis=0, tiled=True)  28.6 us
    dot_general x1, matrix products, on_device(): lax.dot_general(cotangent, lax.all_gather(weight, 'row', axis=1, tiled=Tr...  10.6 us
  transfers between devices with their start and end apart: 3, of which 3 were waited for; matrix products, arithmetic and copies ran while one was open for 3% of the time, Pallas kernels for 0%

commit v1 on v0

v1 whole, which is shorter than its diff:
```python
import jax
import jax.numpy as jnp
from jax import lax
from jax.experimental import pallas as pl
from jax.experimental.pallas import tpu as pltpu
from jax.sharding import PartitionSpec as P

MESH = pl.DeviceIdType.MESH
NX, NY, NZ = 4, 4, 16
BF16, F32 = jnp.bfloat16, jnp.float32
TOK = 64
WID = 512
PLANE = 2 * TOK
QUARTER = 256
HID = 896


def start_of(q):
    return pl.multiple_of(256 * q - 128 * lax.div(q, 3), 128)


def kernel(
    g_ref, h_ref, w_ref, tok_ref, wgt_ref,
    gf, wq, hq, pst, red, acc, wgs, wgo, tos, too,
    gp_s, gp_r, hx_s, hx_r, w_s, w_r, hy_s, hy_r,
    ring_s, ring_r, sib_s, sib_r, red_s, red_r, wo_s, wo_r, to_s, to_r,
):
    row, col = lax.axis_index("row"), lax.axis_index("col")
    x, y = lax.rem(row, NX), lax.div(row, NX)
    z, k = lax.div(col, 2), lax.rem(col, 2)

    def dev(x_, y_, z_, k_):
        return {"row": y_ * NX + x_, "col": z_ * 2 + k_}

    def xpeer(dx):
        return lax.rem(x + dx, NX)

    def ypeer(dy):
        return lax.rem(y + dy, NY)

    right, left = lax.rem(z + 1, NZ), lax.rem(z + NZ - 1, NZ)
    sibling = dev(x, y, z, 1 - k)

    def remote(src, dst, ss, rs, to):
        return pltpu.make_async_remote_copy(
            src_ref=src, dst_ref=dst, send_sem=ss, recv_sem=rs, device_id=to, device_id_type=MESH
        )

    barrier = pltpu.get_barrier_semaphore()
    partners = [dev(xpeer(d), y, z, k) for d in (1, 2, 3)]
    partners += [dev(x, ypeer(d), z, k) for d in (1, 2, 3)]
    partners += [dev(x, y, right, k), dev(x, y, left, k), sibling]
    for partner in partners:
        pl.semaphore_signal(barrier, inc=1, device_id=partner, device_id_type=MESH)
    pl.semaphore_wait(barrier, len(partners))

    def shard_at(d):
        return gf.at[
            lax.div(d, 2),
            pl.ds(pl.multiple_of(TOK * col, TOK), TOK),
            pl.ds(pl.multiple_of(WID * lax.rem(d, 2), WID), WID),
        ]

    def gp_copy(dx, owner):
        return remote(g_ref, shard_at(owner), gp_s.at[dx - 1], gp_r.at[dx - 1], dev(xpeer(dx), y, z, k))

    def hx_copy(dx, owner):
        to = xpeer(dx)
        return remote(
            h_ref.at[:, pl.ds(start_of(to), QUARTER)],
            hq.at[pl.ds(pl.multiple_of(PLANE * (NX * y + owner), PLANE), PLANE), :],
            hx_s.at[dx - 1], hx_r.at[dx - 1], dev(to, y, z, k),
        )

    def w_copy(dx, owner):
        to = xpeer(dx)
        return remote(
            w_ref.at[pl.ds(start_of(to), QUARTER), :], wq.at[owner],
            w_s.at[dx - 1], w_r.at[dx - 1], dev(to, y, z, k),
        )

    def hy_copy(dy, owner):
        rows = hq.at[pl.ds(pl.multiple_of(NX * PLANE * owner, NX * PLANE), NX * PLANE), :]
        return remote(rows, rows, hy_s.at[dy - 1], hy_r.at[dy - 1], dev(x, ypeer(dy), z, k))

    for dx in (1, 2, 3):
        gp_copy(dx, x).start()
    for dx in (1, 2, 3):
        hx_copy(dx, x).start()
    shard_at(x)[...] = g_ref[...]
    hq[pl.ds(pl.multiple_of(PLANE * row, PLANE), PLANE), :] = h_ref[:, pl.ds(start_of(x), QUARTER)]
    wq[x] = w_ref[pl.ds(start_of(x), QUARTER), :]

    def unit(p, core, h):
        return gf.at[h, pl.ds(pl.multiple_of(TOK * (2 * p + core), TOK), TOK), :]

    def away(direction, s):
        return lax.rem(z + NZ - s, NZ) if direction == 0 else lax.rem(z + s, NZ)

    def hop(direction, s, h):
        block = unit(away(direction, s - 1), k, h)
        to = right if direction == 0 else left
        return remote(block, block, ring_s.at[direction, s - 1, h], ring_r.at[direction, s - 1, h], dev(x, y, to, k))

    def landed(direction, s, h):
        block = unit(away(direction, s), k, h)
        remote(block, block, ring_s.at[direction, s - 1, h], ring_r.at[direction, s - 1, h], sibling).wait_recv()

    def across(p, h):
        block = unit(p, k, h)
        return remote(block, block, sib_s.at[p, h], sib_r.at[p, h], sibling)

    def crossed(p, h):
        block = unit(p, 1 - k, h)
        remote(block, block, sib_s.at[p, h], sib_r.at[p, h], sibling).wait_recv()

    for dx in (1, 2, 3):
        gp_copy(dx, xpeer(NX - dx)).wait_recv()
    for h in (0, 1):
        hop(0, 1, h).start()
        hop(1, 1, h).start()
        across(z, h).start()
    for dx in (1, 2, 3):
        w_copy(dx, x).start()
    for dx in (1, 2, 3):
        hx_copy(dx, xpeer(NX - dx)).wait_recv()
    for dy in (1, 2, 3):
        hy_copy(dy, y).start()

    acc[...] = jnp.zeros_like(acc)

    def service(s, h):
        for direction in (0, 1):
            landed(direction, s, h)
            if h == direction:
                hop(direction, s + 1, h).start()
            else:
                pl.when(s < 7)(lambda: hop(direction, s + 1, h).start())
            across(away(direction, s), h).start()

    def plane_of(n):
        return lax.rem(z + NZ + (1 - 2 * lax.rem(n, 2)) * lax.div(n + 1, 2), NZ)

    def red_copy(p):
        return remote(
            pst.at[p], red.at[y, lax.rem(p, NX)], red_s.at[p], red_r.at[y, lax.rem(p, NX)],
            dev(x, lax.div(p, NX), z, k),
        )

    def compute(n):
        p = plane_of(n)
        for h in (0, 1):
            crossed(p, h)
        rows = pl.ds(pl.multiple_of(PLANE * p, PLANE), PLANE)
        part = None
        for d in range(4):
            term = lax.dot_general(
                gf[d // 2, rows, WID * (d % 2):WID * (d % 2 + 1)], wq[d],
                (((1,), (1,)), ((), ())), preferred_element_type=F32,
            )
            part = term if part is None else part + term
        mine = lax.div(p, NX) == y

        @pl.when(mine)
        def _():
            red[y, lax.rem(p, NX)] = part

        @pl.when(jnp.logical_not(mine))
        def _():
            pst[p] = part
            red_copy(p).start()

        for d in range(4):
            acc[d] += lax.dot_general(
                hq[rows, :], gf[d // 2, rows, WID * (d % 2):WID * (d % 2 + 1)],
                (((0,), (0,)), ((), ())), preferred_element_type=F32,
            )

    def compute_range(lo, hi):
        lax.fori_loop(lo, hi, lambda n, c: (compute(n), c)[1], 0)

    def early(s, c):
        for h in (0, 1):
            service(s, h)
        return c

    lax.fori_loop(1, 3, early, 0)
    for dx in (1, 2, 3):
        w_copy(dx, xpeer(NX - dx)).wait_recv()
    for dy in (1, 2, 3):
        hy_copy(dy, ypeer(NY - dy)).wait_recv()

    def late(s, c):
        for h in (0, 1):
            service(s, h)
            t = 2 * (s - 3) + h
            compute_range(jnp.minimum(2 * t, 2 * s - 3 + h), jnp.minimum(2 * t + 2, 2 * s - 2 + h))
        return c

    lax.fori_loop(3, 8, late, 0)
    far = away(0, 8)
    for direction in (0, 1):
        landed(direction, 8, direction)
        across(far, direction).start()
    compute_range(13, 16)

    def wo_copy(dx, owner):
        to = xpeer(dx)
        return remote(wgs.at[to], wgo.at[owner], wo_s.at[dx - 1], wo_r.at[dx - 1], dev(to, y, z, k))

    def to_copy(dx, owner):
        to = xpeer(dx)
        return remote(tos.at[to], too.at[owner], to_s.at[dx - 1], to_r.at[dx - 1], dev(to, y, z, k))

    for d in range(4):
        wgs[d] = acc[d].astype(BF16)
    for dx in (1, 2, 3):
        wo_copy(dx, x).start()
    wgo[x] = wgs[x]

    for dx in (1, 2, 3, 0):
        xo = xpeer(dx)
        for dy in (1, 2, 3):
            src = ypeer(dy)
            remote(red.at[src, xo], red.at[src, xo], red_s.at[0], red_r.at[src, xo], sibling).wait_recv()
        tos[xo] = (red[0, xo] + red[1, xo] + red[2, xo] + red[3, xo]).astype(BF16)
        if dx:
            to_copy(dx, x).start()
        else:
            too[x] = tos[x]

    for dx in (1, 2, 3):
        to_copy(dx, xpeer(NX - dx)).wait_recv()
    for q in range(3):
        tok_ref[:, QUARTER * q:QUARTER * (q + 1)] = too[q]
    tok_ref[:, 768:] = too[3, :, 128:]
    for dx in (1, 2, 3):
        wo_copy(dx, xpeer(NX - dx)).wait_recv()
    for q in range(3):
        wgt_ref[QUARTER * q:QUARTER * (q + 1), :] = wgo[q]
    wgt_ref[768:, :] = wgo[3, 128:, :]

    for dx in (1, 2, 3):
        gp_copy(dx, x).wait_send()
        hx_copy(dx, x).wait_send()
        w_copy(dx, x).wait_send()
        hy_copy(dx, y).wait_send()
        wo_copy(dx, x).wait_send()
        to_copy(dx, x).wait_send()

    def drain(s, c):
        for h in (0, 1):
            hop(0, s, h).wait_send()
            hop(1, s, h).wait_send()
        return c

    lax.fori_loop(1, 8, drain, 0)
    hop(0, 8, 0).wait_send()
    hop(1, 8, 1).wait_send()

    def drain_planes(p, c):
        for h in (0, 1):
            across(p, h).wait_send()
        pl.when(lax.div(p, NX) != y)(lambda: red_copy(p).wait_send())
        return c

    lax.fori_loop(0, NZ, drain_planes, 0)


def on_device(out_grad, hidden, weight):
    dma = pltpu.SemaphoreType.DMA
    vmem = pl.BlockSpec(memory_space=pltpu.VMEM)
    return pl.pallas_call(
        kernel,
        out_shape=(
            jax.ShapeDtypeStruct((PLANE, HID), BF16),
            jax.ShapeDtypeStruct((HID, WID), BF16),
        ),
        in_specs=[vmem] * 3,
        out_specs=(vmem, vmem),
        scratch_shapes=[
            pltpu.VMEM((2, NZ * PLANE, 2 * WID), BF16),
            pltpu.VMEM((4, QUARTER, WID), BF16),
            pltpu.VMEM((NZ * PLANE, QUARTER), BF16),
            pltpu.VMEM((NZ, PLANE, QUARTER), F32),
            pltpu.VMEM((NY, NX, PLANE, QUARTER), F32),
            pltpu.VMEM((4, QUARTER, WID), F32),
            pltpu.VMEM((4, QUARTER, WID), BF16),
            pltpu.VMEM((4, QUARTER, WID), BF16),
            pltpu.VMEM((4, PLANE, QUARTER), BF16),
            pltpu.VMEM((4, PLANE, QUARTER), BF16),
            *[dma((3,))] * 8,
            dma((2, 8, 2)), dma((2, 8, 2)),
            dma((NZ, 2)), dma((NZ, 2)),
            dma((NZ,)), dma((NY, NX)),
            *[dma((3,))] * 4,
        ],
        compiler_params=pltpu.CompilerParams(
            collective_id=0, has_side_effects=True, vmem_limit_bytes=48 * 2**20
        ),
    )(out_grad, hidden, weight)


def solution(mesh):
    return jax.shard_map(
        on_device,
        mesh=mesh,
        in_specs=(P("col", "row"), P("row", "col"), P("col", "row")),
        out_specs=(P("row", "col"), P("col", "row")),
        check_vma=False,
    )
```

time: 301 us -> 91.6 us (0.30)
  the two profiles are of different devices: /device:TPU:1 before, /device:TPU:16 now
where the time goes in v1:
time: 91.6 us; the launch traced here: 91.4 us
  Pallas kernels  86.2 us (94%)
  local copies, waits for them, and re-layouts  4.56 us (5%)
    pallas_call x1, Pallas kernels, on_device(): pl.pallas_call(kernel, out_shape=(jax.ShapeDtypeStruct((PLANE, HID), BF16...  86.2 us
    unnamed x8, local copies, waits for them, and re-layouts  4.56 us

profile of v1, /device:TPU:16, one launch (start us, length us, event | category | flops | bytes accessed | tf_op | source)
XLA Modules:
  0.0 91.4 jit_solution(9516534118816573796)
XLA Ops:
  0.6 0.0 copy-start
  0.6 1.2 %copy-done = bf16[896,512]{1,0:T(8,128)(2,1)S(1)} copy-done((bf16[896,512]{1,0:T(8,128)(2,1)S(1)}, bf16[896,512]{1,0:T(8,128)(2,1)}, u32[]{:S(2)}) %copy-start) | copy-done | bytes 917528
  1.8 0.0 copy-start.1
  1.8 0.9 %copy-done.1 = bf16[128,896]{1,0:T(8,128)(2,1)S(1)} copy-done((bf16[128,896]{1,0:T(8,128)(2,1)S(1)}, bf16[128,896]{1,0:T(8,128)(2,1)}, u32[]{:S(2)}) %copy-start.1) | copy-done | bytes 229400
  2.7 0.0 copy-start.2
  2.8 0.8 copy-done.2
  3.6 86.2 %shard_map.50 = (bf16[128,896]{1,0:T(8,128)(2,1)S(1)}, bf16[896,512]{1,0:T(8,128)(2,1)S(1)}) custom-call(bf16[64,512]{1,0:T(8,128)(2,1)S(1)} %copy-done.2, bf16[128,896]{1,0:T(8,128)(2,1)S(1)} %copy-done.1, bf16[896,512]{1,0:T(8,128)(2,1)S(1)} %copy-done), custom_call_target="tpu_custom_call" | custom-call | tf_op jit(solution)/shard_map/pallas_call | solution.py:273
  89.8 0.7 copy.7
  90.5 0.9 %copy.8 = bf16[896,512]{1,0:T(8,128)(2,1)} copy(bf16[896,512]{1,0:T(8,128)(2,1)S(1)} %get-tuple-element.5) | data formatting | bytes 1835008
Async XLA Ops:
  0.6 1.2 %copy-start = (bf16[896,512]{1,0:T(8,128)(2,1)S(1)}, bf16[896,512]{1,0:T(8,128)(2,1)}, u32[]{:S(2)}) copy-start(bf16[896,512]{1,0:T(8,128)(2,1)} %w_ref.1) | copy-start | bytes 2752516
  1.8 0.9 %copy-start.1 = (bf16[128,896]{1,0:T(8,128)(2,1)S(1)}, bf16[128,896]{1,0:T(8,128)(2,1)}, u32[]{:S(2)}) copy-start(bf16[128,896]{1,0:T(8,128)(2,1)} %h_ref.1) | copy-start | bytes 688132
  2.7 0.8 copy-start.2

commit v2 on v0

v2 whole, which is shorter than its diff:
```python
import jax
import jax.numpy as jnp
from jax import lax
from jax.experimental import pallas as pl
from jax.experimental.pallas import tpu as pltpu
from jax.sharding import PartitionSpec as P

MESH = pl.DeviceIdType.MESH
NX, NY, NZ = 4, 4, 16
BF16, F32 = jnp.bfloat16, jnp.float32
TOK = 64
WID = 512
PLANE = 2 * TOK
QUARTER = 256
HID = 896
HEAD = 16
SLICE = 32
SPREAD, PER = 2, 2


def start_of(q):
    return pl.multiple_of(256 * q - 128 * lax.div(q, 3), 128)


def kernel(
    g_ref, h_ref, w_ref, tok_ref, wgt_ref,
    gf, wq, hf, pst, red, tos, too,
    own, gp_s, gp_r, a1_s, a1_r, b1_s, b1_r, w_s, w_r, a2_s, a2_r, b2_s, b2_r,
    ring_s, ring_r, sib_s, sib_r, red_s, red_r, to_s, to_r,
):
    row, col = lax.axis_index("row"), lax.axis_index("col")
    x, y = lax.rem(row, NX), lax.div(row, NX)
    z, k = lax.div(col, 2), lax.rem(col, 2)

    def dev(x_, y_, z_, k_):
        return {"row": y_ * NX + x_, "col": z_ * 2 + k_}

    def xpeer(dx):
        return lax.rem(x + dx, NX)

    def ypeer(dy):
        return lax.rem(y + dy, NY)

    right, left = lax.rem(z + 1, NZ), lax.rem(z + NZ - 1, NZ)
    sibling = dev(x, y, z, 1 - k)

    def rows(i, n):
        return pl.ds(pl.multiple_of(n * i, n), n)

    def remote(src, dst, ss, rs, to):
        return pltpu.make_async_remote_copy(
            src_ref=src, dst_ref=dst, send_sem=ss, recv_sem=rs, device_id=to, device_id_type=MESH
        )

    def head(p):
        return hf.at[pl.ds(pl.multiple_of(PLANE * p, PLANE), HEAD), :]

    def rest(p):
        return hf.at[pl.ds(pl.multiple_of(PLANE * p + HEAD, 16), PLANE - HEAD), :]

    locals_ = [
        pltpu.make_async_copy(g_ref, gf.at[x, rows(col, TOK), :], own.at[0]),
        pltpu.make_async_copy(w_ref.at[pl.ds(start_of(x), QUARTER), :], wq.at[x], own.at[1]),
        pltpu.make_async_copy(h_ref.at[pl.ds(0, HEAD), :], head(row), own.at[2]),
        pltpu.make_async_copy(h_ref.at[pl.ds(HEAD, PLANE - HEAD), :], rest(row), own.at[3]),
    ]
    for copy in locals_:
        copy.start()

    barrier = pltpu.get_barrier_semaphore()
    partners = [dev(x, y, right, k), dev(x, y, left, k), sibling]
    partners += [dev(xpeer(d), ypeer(e), z, k) for d in range(4) for e in range(4) if d or e]
    for partner in partners:
        pl.semaphore_signal(barrier, inc=1, device_id=partner, device_id_type=MESH)
    locals_[0].wait()
    pl.semaphore_wait(barrier, len(partners))

    def gp_copy(dx, owner):
        return remote(
            g_ref, gf.at[owner, rows(col, TOK), :], gp_s.at[dx - 1], gp_r.at[dx - 1], dev(xpeer(dx), y, z, k)
        )

    def w_copy(dx, owner):
        to = xpeer(dx)
        return remote(
            w_ref.at[pl.ds(start_of(to), QUARTER), :], wq.at[owner],
            w_s.at[dx - 1], w_r.at[dx - 1], dev(to, y, z, k),
        )

    def a1_copy(dx, owner):
        return remote(
            h_ref.at[pl.ds(0, HEAD), :], head(NX * y + owner),
            a1_s.at[dx - 1], a1_r.at[dx - 1], dev(xpeer(dx), y, z, k),
        )

    def a2_copy(dy, owner, i):
        block = head(NX * owner + i)
        return remote(block, block, a2_s.at[dy - 1, i], a2_r.at[dy - 1, i], dev(x, ypeer(dy), z, k))

    def b1_copy(dy, owner):
        return remote(
            h_ref.at[pl.ds(HEAD, PLANE - HEAD), :], rest(NX * owner + x),
            b1_s.at[dy - 1], b1_r.at[dy - 1], dev(x, ypeer(dy), z, k),
        )

    def b2_copy(dx, owner, i):
        block = rest(NX * i + owner)
        return remote(block, block, b2_s.at[dx - 1, i], b2_r.at[dx - 1, i], dev(xpeer(dx), y, z, k))

    def unit(p, core, j):
        return gf.at[xpeer(j), rows(2 * p + core, TOK), :]

    def away(direction, s):
        return lax.rem(z + NZ - s, NZ) if direction == 0 else lax.rem(z + s, NZ)

    def hop(direction, s, j):
        block = unit(away(direction, s - 1), k, j)
        to = right if direction == 0 else left
        return remote(block, block, ring_s.at[direction, s - 1, j], ring_r.at[direction, s - 1, j], dev(x, y, to, k))

    def landed(direction, s, j):
        block = unit(away(direction, s), k, j)
        remote(block, block, ring_s.at[direction, s - 1, j], ring_r.at[direction, s - 1, j], sibling).wait_recv()

    def across(p, j):
        block = unit(p, k, j)
        return remote(block, block, sib_s.at[p, j], sib_r.at[p, j], sibling)

    def crossed(p, j):
        block = unit(p, 1 - k, j)
        remote(block, block, sib_s.at[p, j], sib_r.at[p, j], sibling).wait_recv()

    for dx in (1, 2, 3):
        gp_copy(dx, x).start()
    for j in range(4):
        if j:
            gp_copy(NX - j, xpeer(j)).wait_recv()
        hop(0, 1, j).start()
        hop(1, 1, j).start()
        across(z, j).start()
        if j == 0:
            for d in (1, 2, 3):
                b1_copy(d, y).start()
    for d in (1, 2, 3):
        a1_copy(d, x).start()
    for d in (1, 2, 3):
        w_copy(d, x).start()

    def service(s, j):
        for direction in (0, 1):
            landed(direction, s, j)
            if j // 2 == direction:
                hop(direction, s + 1, j).start()
            elif s < 7:
                hop(direction, s + 1, j).start()
            across(away(direction, s), j).start()

    def plane_of(n):
        return lax.rem(z + NZ + (1 - 2 * lax.rem(n, 2)) * lax.div(n + 1, 2), NZ)

    def red_copy(p, dy):
        return remote(
            pst.at[p, rows(ypeer(dy), SLICE), :], red.at[dy - 1, p],
            red_s.at[p, dy - 1], red_r.at[p, dy - 1], dev(x, ypeer(dy), z, k),
        )

    def token_part(n):
        p = plane_of(n)
        for j in range(4):
            crossed(p, j)
        part = None
        for d in range(4):
            term = lax.dot_general(
                gf[d, rows(p, PLANE), :], wq[d], (((1,), (1,)), ((), ())), preferred_element_type=F32
            )
            part = term if part is None else part + term
        pst[p] = part
        for dy in (1, 2, 3):
            red_copy(p, dy).start()

    def to_copy(p, x_, y_):
        return remote(
            tos.at[p], too.at[x_, rows(y_, SLICE), :],
            to_s.at[p], to_r.at[x_, y_], dev(lax.rem(p, NX), lax.div(p, NX), z, k),
        )

    def finish(n):
        p = plane_of(n)
        for dy in (1, 2, 3):
            red_copy(p, dy).wait_recv()
        tos[p] = (pst[p, rows(y, SLICE), :] + red[0, p] + red[1, p] + red[2, p]).astype(BF16)

        @pl.when(p == row)
        def _():
            too[x, rows(y, SLICE), :] = tos[p]

        @pl.when(p != row)
        def _():
            to_copy(p, x, y).start()

    def weight_all():
        for d in (1, 2, 3):
            for i in range(4):
                a2_copy(d, ypeer(NY - d), i).wait_recv()
                b2_copy(d, xpeer(NX - d), i).wait_recv()
        for lo, hi in ((0, 256), (256, 512), (512, 768), (768, 896)):
            total = lax.dot_general(
                hf[:, lo:hi], gf[x], (((0,), (0,)), ((), ())), preferred_element_type=F32
            )
            wgt_ref[lo:hi, :] = total.astype(BF16)

    def each(part, lo, hi):
        lax.fori_loop(lo, hi, lambda n, c: (part(n), c)[1], 0)

    def step(s, *bodies):
        for j in range(4):
            service(s, j)
            for body in bodies:
                body(j)

    def spread(s):
        def body(j):
            m = 4 * (s - SPREAD) + j
            for i in range(PER * m, PER * (m + 1)):
                if i < 12:
                    a2_copy(i % 3 + 1, y, i // 3).start()
                    b2_copy(i % 3 + 1, x, i // 3).start()

        return body

    def plan(part, *ranges):
        def body(j):
            lo, hi = ranges[j]
            if hi > lo:
                each(part, lo, hi)

        return body

    none = (0, 0)
    step(1)
    for copy in locals_[2:]:
        copy.wait()
    for d in (1, 2, 3):
        b1_copy(d, ypeer(NY - d)).wait_recv()
        a1_copy(d, xpeer(NX - d)).wait_recv()
    step(2, spread(2))
    locals_[1].wait()
    for d in (1, 2, 3):
        w_copy(d, xpeer(NX - d)).wait_recv()
    step(3, spread(3), plan(token_part, (0, 1), (1, 2), (2, 3), (3, 4)))
    step(4, spread(4), plan(token_part, (4, 5), (5, 6), (6, 7), none))
    step(5, spread(5), plan(token_part, none, (7, 8), none, (8, 9)), plan(finish, (0, 3), none, (3, 5), none))
    step(6, spread(6), plan(token_part, none, (9, 10), none, (10, 11)), plan(finish, (5, 7), none, (7, 9), none))
    step(7, spread(7), plan(token_part, none, (11, 12), none, (12, 13)), plan(finish, (9, 10), none, (10, 11), none))
    far = away(0, 8)
    for direction in (0, 1):
        for j in (2 * direction, 2 * direction + 1):
            landed(direction, 8, j)
            across(far, j).start()
    each(token_part, 13, 15)
    each(token_part, 15, 16)
    each(finish, 11, 13)
    weight_all()
    each(finish, 13, 16)

    def arrived(i, c):
        pl.when(i != row)(lambda: to_copy(0, lax.rem(i, NX), lax.div(i, NX)).wait_recv())
        return c

    lax.fori_loop(0, NX * NY, arrived, 0)
    for q in range(3):
        tok_ref[:, QUARTER * q:QUARTER * (q + 1)] = too[q]
    tok_ref[:, 768:] = too[3, :, 128:]

    for d in (1, 2, 3):
        gp_copy(d, x).wait_send()
        w_copy(d, x).wait_send()
        a1_copy(d, x).wait_send()
        b1_copy(d, y).wait_send()
        for i in range(4):
            a2_copy(d, y, i).wait_send()
            b2_copy(d, x, i).wait_send()

    def drain(s, c):
        for j in range(4):
            hop(0, s, j).wait_send()
            hop(1, s, j).wait_send()
        return c

    lax.fori_loop(1, 8, drain, 0)
    for j in (0, 1):
        hop(0, 8, j).wait_send()
        hop(1, 8, 2 + j).wait_send()

    def drain_planes(p, c):
        for j in range(4):
            across(p, j).wait_send()
        for dy in (1, 2, 3):
            red_copy(p, dy).wait_send()
        pl.when(p != row)(lambda: to_copy(p, x, y).wait_send())
        return c

    lax.fori_loop(0, NZ, drain_planes, 0)


def on_device(out_grad, hidden, weight):
    dma = pltpu.SemaphoreType.DMA
    vmem = pl.BlockSpec(memory_space=pltpu.VMEM)
    return pl.pallas_call(
        kernel,
        out_shape=(
            jax.ShapeDtypeStruct((PLANE, HID), BF16),
            jax.ShapeDtypeStruct((HID, WID), BF16),
        ),
        in_specs=[pl.BlockSpec(memory_space=pl.ANY)] * 3,
        out_specs=(vmem, vmem),
        scratch_shapes=[
            pltpu.VMEM((4, NZ * PLANE, WID), BF16),
            pltpu.VMEM((4, QUARTER, WID), BF16),
            pltpu.VMEM((NZ * PLANE, HID), BF16),
            pltpu.VMEM((NZ, PLANE, QUARTER), F32),
            pltpu.VMEM((NY - 1, NZ, SLICE, QUARTER), F32),
            pltpu.VMEM((NZ, SLICE, QUARTER), BF16),
            pltpu.VMEM((4, PLANE, QUARTER), BF16),
            dma((4,)),
            *[dma((3,))] * 8,
            *[dma((3, 4))] * 4,
            dma((2, 8, 4)), dma((2, 8, 4)),
            dma((NZ, 4)), dma((NZ, 4)),
            dma((NZ, 3)), dma((NZ, 3)),
            dma((NZ,)), dma((NX, NY)),
        ],
        compiler_params=pltpu.CompilerParams(
            collective_id=0, has_side_effects=True, vmem_limit_bytes=48 * 2**20
        ),
    )(out_grad, hidden, weight)


def solution(mesh):
    return jax.shard_map(
        on_device,
        mesh=mesh,
        in_specs=(P("col", "row"), P("row", "col"), P("col", "row")),
        out_specs=(P("row", "col"), P("col", "row")),
        check_vma=False,
    )
```

time: 301 us -> 84.8 us (0.28)
  the two profiles are of different devices: /device:TPU:1 before, /device:TPU:16 now
where the time goes in v2:
time: 84.8 us; the launch traced here: 84.5 us
  Pallas kernels  79.3 us (94%)
  local copies, waits for them, and re-layouts  4.56 us (5%)
    pallas_call x1, Pallas kernels, on_device(): pl.pallas_call(kernel, out_shape=(jax.ShapeDtypeStruct((PLANE, HID), BF16...  79.3 us
    unnamed x8, local copies, waits for them, and re-layouts  4.56 us

profile of v2, /device:TPU:16, one launch (start us, length us, event | category | flops | bytes accessed | tf_op | source)
XLA Modules:
  0.0 84.5 jit_solution(6925135107812842959)
XLA Ops:
  0.6 0.0 copy-start
  0.6 1.2 %copy-done = bf16[896,512]{1,0:T(8,128)(2,1)S(1)} copy-done((bf16[896,512]{1,0:T(8,128)(2,1)S(1)}, bf16[896,512]{1,0:T(8,128)(2,1)}, u32[]{:S(2)}) %copy-start) | copy-done | bytes 917528
  1.8 0.0 copy-start.1
  1.8 0.9 %copy-done.1 = bf16[128,896]{1,0:T(8,128)(2,1)S(1)} copy-done((bf16[128,896]{1,0:T(8,128)(2,1)S(1)}, bf16[128,896]{1,0:T(8,128)(2,1)}, u32[]{:S(2)}) %copy-start.1) | copy-done | bytes 229400
  2.7 0.0 copy-start.2
  2.8 0.8 copy-done.2
  3.6 79.3 %shard_map.50 = (bf16[128,896]{1,0:T(8,128)(2,1)S(1)}, bf16[896,512]{1,0:T(8,128)(2,1)S(1)}) custom-call(bf16[64,512]{1,0:T(8,128)(2,1)S(1)} %copy-done.2, bf16[128,896]{1,0:T(8,128)(2,1)S(1)} %copy-done.1, bf16[896,512]{1,0:T(8,128)(2,1)S(1)} %copy-done), custom_call_target="tpu_custom_call" | custom-call | tf_op jit(solution)/shard_map/pallas_call | solution.py:309
  82.9 0.7 copy.7
  83.6 0.9 %copy.8 = bf16[896,512]{1,0:T(8,128)(2,1)} copy(bf16[896,512]{1,0:T(8,128)(2,1)S(1)} %get-tuple-element.5) | data formatting | bytes 1835008
Async XLA Ops:
  0.6 1.2 %copy-start = (bf16[896,512]{1,0:T(8,128)(2,1)S(1)}, bf16[896,512]{1,0:T(8,128)(2,1)}, u32[]{:S(2)}) copy-start(bf16[896,512]{1,0:T(8,128)(2,1)} %w_ref.1) | copy-start | bytes 2752516
  1.8 0.9 %copy-start.1 = (bf16[128,896]{1,0:T(8,128)(2,1)S(1)}, bf16[128,896]{1,0:T(8,128)(2,1)}, u32[]{:S(2)}) copy-start(bf16[128,896]{1,0:T(8,128)(2,1)} %h_ref.1) | copy-start | bytes 688132
  2.7 0.8 copy-start.2

commit v3 on v2

--- a/solution.py
+++ b/solution.py
@@ -198,12 +198,13 @@
         def _():
             to_copy(p, x, y).start()
 
-    def weight_all():
+    def hidden_here():
         for d in (1, 2, 3):
             for i in range(4):
                 a2_copy(d, ypeer(NY - d), i).wait_recv()
                 b2_copy(d, xpeer(NX - d), i).wait_recv()
-        for lo, hi in ((0, 256), (256, 512), (512, 768), (768, 896)):
+    def weight_part(*chunks):
+        for lo, hi in chunks:
             total = lax.dot_general(
                 hf[:, lo:hi], gf[x], (((0,), (0,)), ((), ())), preferred_element_type=F32
             )
@@ -244,11 +245,11 @@
         b1_copy(d, ypeer(NY - d)).wait_recv()
         a1_copy(d, xpeer(NX - d)).wait_recv()
     step(2, spread(2))
+    step(3, spread(3))
     locals_[1].wait()
     for d in (1, 2, 3):
         w_copy(d, xpeer(NX - d)).wait_recv()
-    step(3, spread(3), plan(token_part, (0, 1), (1, 2), (2, 3), (3, 4)))
-    step(4, spread(4), plan(token_part, (4, 5), (5, 6), (6, 7), none))
+    step(4, plan(token_part, (0, 2), (2, 4), (4, 6), (6, 7)))
     step(5, spread(5), plan(token_part, none, (7, 8), none, (8, 9)), plan(finish, (0, 3), none, (3, 5), none))
     step(6, spread(6), plan(token_part, none, (9, 10), none, (10, 11)), plan(finish, (5, 7), none, (7, 9), none))
     step(7, spread(7), plan(token_part, none, (11, 12), none, (12, 13)), plan(finish, (9, 10), none, (10, 11), none))
@@ -260,8 +261,10 @@
     each(token_part, 13, 15)
     each(token_part, 15, 16)
     each(finish, 11, 13)
-    weight_all()
+    hidden_here()
+    weight_part((0, 256), (256, 512))
     each(finish, 13, 16)
+    weight_part((512, 768), (768, 896))
 
     def arrived(i, c):
         pl.when(i != row)(lambda: to_copy(0, lax.rem(i, NX), lax.div(i, NX)).wait_recv())
@@ -312,7 +315,7 @@
             jax.ShapeDtypeStruct((PLANE, HID), BF16),
             jax.ShapeDtypeStruct((HID, WID), BF16),
         ),
-        in_specs=[pl.BlockSpec(memory_space=pl.ANY)] * 3,
+        in_specs=[pl.BlockSpec(memory_space=pltpu.HBM)] * 3,
         out_specs=(vmem, vmem),
         scratch_shapes=[
             pltpu.VMEM((4, NZ * PLANE, WID), BF16),
@@ -331,7 +334,7 @@
             dma((NZ,)), dma((NX, NY)),
         ],
         compiler_params=pltpu.CompilerParams(
-            collective_id=0, has_side_effects=True, vmem_limit_bytes=48 * 2**20
+            collective_id=0, has_side_effects=True, vmem_limit_bytes=53000 * 1024
         ),
     )(out_grad, hidden, weight)
 

time: 84.8 us -> 83.7 us (0.987)
  local copies, waits for them, and re-layouts: 4.56 us -> 3.38 us
    unnamed x8 -> x6, local copies, waits for them, and re-layouts: 4.56 us -> 3.38 us
where the time goes in v3:
time: 83.7 us; the launch traced here: 83.5 us
  Pallas kernels  79.5 us (95%)
  local copies, waits for them, and re-layouts  3.38 us (4%)
    pallas_call x1, Pallas kernels, on_device(): pl.pallas_call(kernel, out_shape=(jax.ShapeDtypeStruct((PLANE, HID), BF16...  79.5 us
    unnamed x6, local copies, waits for them, and re-layouts  3.38 us

profile of v3, /device:TPU:16, one launch (start us, length us, event | category | flops | bytes accessed | tf_op | source)
XLA Modules:
  0.0 83.5 jit_solution(16276927763192045605)
XLA Ops:
  0.6 0.0 copy-start
  0.6 0.9 %copy-done = bf16[128,896]{1,0:T(8,128)(2,1)S(1)} copy-done((bf16[128,896]{1,0:T(8,128)(2,1)S(1)}, bf16[128,896]{1,0:T(8,128)(2,1)}, u32[]{:S(2)}) %copy-start) | copy-done | bytes 229400
  1.6 0.0 copy-start.1
  1.6 0.8 %copy-done.1 = bf16[64,512]{1,0:T(8,128)(2,1)S(1)} copy-done((bf16[64,512]{1,0:T(8,128)(2,1)S(1)}, bf16[64,512]{1,0:T(8,128)(2,1)}, u32[]{:S(2)}) %copy-start.1) | copy-done | bytes 65560
  2.4 79.5 %shard_map.50 = (bf16[128,896]{1,0:T(8,128)(2,1)S(1)}, bf16[896,512]{1,0:T(8,128)(2,1)S(1)}) custom-call(bf16[64,512]{1,0:T(8,128)(2,1)S(1)} %copy-done.1, bf16[128,896]{1,0:T(8,128)(2,1)S(1)} %copy-done, bf16[896,512]{1,0:T(8,128)(2,1)} %w_ref.1), custom_call_target="tpu_custom_call" | custom-call | tf_op jit(solution)/shard_map/pallas_call | solution.py:312
  81.9 0.7 copy.7
  82.6 0.9 %copy.8 = bf16[896,512]{1,0:T(8,128)(2,1)} copy(bf16[896,512]{1,0:T(8,128)(2,1)S(1)} %get-tuple-element.5) | data formatting | bytes 1835008
Async XLA Ops:
  0.6 0.9 %copy-start = (bf16[128,896]{1,0:T(8,128)(2,1)S(1)}, bf16[128,896]{1,0:T(8,128)(2,1)}, u32[]{:S(2)}) copy-start(bf16[128,896]{1,0:T(8,128)(2,1)} %h_ref.1) | copy-start | bytes 688132
  1.6 0.8 %copy-start.1 = (bf16[64,512]{1,0:T(8,128)(2,1)S(1)}, bf16[64,512]{1,0:T(8,128)(2,1)}, u32[]{:S(2)}) copy-start(bf16[64,512]{1,0:T(8,128)(2,1)} %g_ref.1) | copy-start | bytes 196612

commit v4 on v3

--- a/solution.py
+++ b/solution.py
@@ -253,6 +253,23 @@
     step(5, spread(5), plan(token_part, none, (7, 8), none, (8, 9)), plan(finish, (0, 3), none, (3, 5), none))
     step(6, spread(6), plan(token_part, none, (9, 10), none, (10, 11)), plan(finish, (5, 7), none, (7, 9), none))
     step(7, spread(7), plan(token_part, none, (11, 12), none, (12, 13)), plan(finish, (9, 10), none, (10, 11), none))
+    def drain_hops(s, c):
+        for j in range(4):
+            hop(0, s, j).wait_send()
+            hop(1, s, j).wait_send()
+        return c
+
+    def sent(n):
+        p = plane_of(n)
+        for j in range(4):
+            across(p, j).wait_send()
+        for dy in (1, 2, 3):
+            red_copy(p, dy).wait_send()
+
+    def told(n):
+        p = plane_of(n)
+        pl.when(p != row)(lambda: to_copy(p, x, y).wait_send())
+
     far = away(0, 8)
     for direction in (0, 1):
         for j in (2 * direction, 2 * direction + 1):
@@ -265,16 +282,6 @@
     weight_part((0, 256), (256, 512))
     each(finish, 13, 16)
     weight_part((512, 768), (768, 896))
-
-    def arrived(i, c):
-        pl.when(i != row)(lambda: to_copy(0, lax.rem(i, NX), lax.div(i, NX)).wait_recv())
-        return c
-
-    lax.fori_loop(0, NX * NY, arrived, 0)
-    for q in range(3):
-        tok_ref[:, QUARTER * q:QUARTER * (q + 1)] = too[q]
-    tok_ref[:, 768:] = too[3, :, 128:]
-
     for d in (1, 2, 3):
         gp_copy(d, x).wait_send()
         w_copy(d, x).wait_send()
@@ -283,27 +290,26 @@
         for i in range(4):
             a2_copy(d, y, i).wait_send()
             b2_copy(d, x, i).wait_send()
-
-    def drain(s, c):
-        for j in range(4):
-            hop(0, s, j).wait_send()
-            hop(1, s, j).wait_send()
-        return c
-
-    lax.fori_loop(1, 8, drain, 0)
+    lax.fori_loop(1, 7, drain_hops, 0)
+    each(sent, 0, 11)
+    each(told, 0, 9)
+    lax.fori_loop(7, 8, drain_hops, 0)
     for j in (0, 1):
         hop(0, 8, j).wait_send()
         hop(1, 8, 2 + j).wait_send()
-
-    def drain_planes(p, c):
-        for j in range(4):
-            across(p, j).wait_send()
-        for dy in (1, 2, 3):
-            red_copy(p, dy).wait_send()
-        pl.when(p != row)(lambda: to_copy(p, x, y).wait_send())
+    each(sent, 11, 16)
+    each(told, 9, 11)
+
+    def arrived(i, c):
+        pl.when(i != row)(lambda: to_copy(0, lax.rem(i, NX), lax.div(i, NX)).wait_recv())
         return c
 
-    lax.fori_loop(0, NZ, drain_planes, 0)
+    lax.fori_loop(0, NX * NY, arrived, 0)
+    for q in range(3):
+        tok_ref[:, QUARTER * q:QUARTER * (q + 1)] = too[q]
+    tok_ref[:, 768:] = too[3, :, 128:]
+
+    each(told, 11, 16)
 
 
 def on_device(out_grad, hidden, weight):

time: 83.7 us -> 83.4 us (level)
  no operation moved by 1% of the time
where the time goes in v4:
time: 83.4 us; the launch traced here: 83.2 us
  Pallas kernels  79.1 us (95%)
  local copies, waits for them, and re-layouts  3.38 us (4%)
    pallas_call x1, Pallas kernels, on_device(): pl.pallas_call(kernel, out_shape=(jax.ShapeDtypeStruct((PLANE, HID), BF16...  79.1 us
    unnamed x6, local copies, waits for them, and re-layouts  3.38 us

profile of v4, /device:TPU:16, one launch (start us, length us, event | category | flops | bytes accessed | tf_op | source)
XLA Modules:
  0.0 83.2 jit_solution(122115547668601051)
XLA Ops:
  0.6 0.0 copy-start
  0.6 0.9 %copy-done = bf16[128,896]{1,0:T(8,128)(2,1)S(1)} copy-done((bf16[128,896]{1,0:T(8,128)(2,1)S(1)}, bf16[128,896]{1,0:T(8,128)(2,1)}, u32[]{:S(2)}) %copy-start) | copy-done | bytes 229400
  1.6 0.0 copy-start.1
  1.6 0.8 %copy-done.1 = bf16[64,512]{1,0:T(8,128)(2,1)S(1)} copy-done((bf16[64,512]{1,0:T(8,128)(2,1)S(1)}, bf16[64,512]{1,0:T(8,128)(2,1)}, u32[]{:S(2)}) %copy-start.1) | copy-done | bytes 65560
  2.4 79.1 %shard_map.50 = (bf16[128,896]{1,0:T(8,128)(2,1)S(1)}, bf16[896,512]{1,0:T(8,128)(2,1)S(1)}) custom-call(bf16[64,512]{1,0:T(8,128)(2,1)S(1)} %copy-done.1, bf16[128,896]{1,0:T(8,128)(2,1)S(1)} %copy-done, bf16[896,512]{1,0:T(8,128)(2,1)} %w_ref.1), custom_call_target="tpu_custom_call" | custom-call | tf_op jit(solution)/shard_map/pallas_call | solution.py:318
  81.5 0.7 copy.7
  82.2 0.9 %copy.8 = bf16[896,512]{1,0:T(8,128)(2,1)} copy(bf16[896,512]{1,0:T(8,128)(2,1)S(1)} %get-tuple-element.5) | data formatting | bytes 1835008
Async XLA Ops:
  0.6 0.9 %copy-start = (bf16[128,896]{1,0:T(8,128)(2,1)S(1)}, bf16[128,896]{1,0:T(8,128)(2,1)}, u32[]{:S(2)}) copy-start(bf16[128,896]{1,0:T(8,128)(2,1)} %h_ref.1) | copy-start | bytes 688132
  1.6 0.8 %copy-start.1 = (bf16[64,512]{1,0:T(8,128)(2,1)S(1)}, bf16[64,512]{1,0:T(8,128)(2,1)}, u32[]{:S(2)}) copy-start(bf16[64,512]{1,0:T(8,128)(2,1)} %g_ref.1) | copy-start | bytes 196612
